TPU v7x, 512 devices: a whole 4x8x8 slice. The times are simulated.
512 devices in a mesh: replica: 8 (over y_lo, core), shard: 64 (over z, y_hi, x).
Axes of the slice: x: 4, y: 8 (y_hi: 2, y_lo: 4; y = y_hi * 4 + y_lo), z: 8, core: 2. Of those that a mesh axis runs over, the one named last changes fastest.
Arguments:
- gradients: bfloat16 [8, 2, 64, 1024, 256], P('replica', None, None, 'shard'), may hold values from -36 to 36
- momentum: float32 [8, 64, 1024, 256], P('replica', None, 'shard'), may hold values from -3 to 3
- params: float32 [64, 1024, 256], P(None, ('shard', 'replica')), may hold values from -6 to 6
- outer_moment: float32 [64, 1024, 256], P(None, ('shard', 'replica')), may hold values from -2 to 2
- shadow: float32 [64, 1024, 256], P(None, ('shard', 'replica')), may hold values from -6 to 6
Outputs:
- new_params: float32 [64, 1024, 256], P(None, ('shard', 'replica'))
- new_outer_moment: float32 [64, 1024, 256], P(None, ('shard', 'replica'))
- new_shadow: float32 [64, 1024, 256], P(None, ('shard', 'replica'))
- new_momentum: float32 [8, 64, 1024, 256], P('replica', None, 'shard')
All inputs are finite; a program needn't handle non-finite values.
Results may differ from a plain program's by a relative error of at most 0.0085.
Values may be sent and summed in bfloat16 or wider, within the bound.
A program may use at most 64 MiB of HBM per device.

v0:
```python
import math
import jax
import jax.numpy as jnp
from jax import lax
from jax.sharding import PartitionSpec as P

D = 1024
INNER = 2
NS_ITERS = 5
quintic_a = 3.4445
quintic_b = -4.775
quintic_c = 2.0315
inner_beta = 0.95
outer_mu = 0.9
outer_rate = 0.7
shadow_decay = 0.9


def split_up(shard, dim, size):
    before, after = (shard.shape[:dim], shard.shape[dim + 1 :])
    return jnp.moveaxis(shard.reshape(*before, size, -1, *after), dim, 0)


def sum_at_owner(shard, axis, dim):
    size = lax.axis_size(axis)
    tiles = lax.all_to_all(split_up(shard, dim, size), axis, 0, 0, tiled=True)
    return jnp.sum(tiles.astype(jnp.float32), axis=0)


def newton_schulz(blocks):
    squares = jnp.sum(jnp.square(blocks.astype(jnp.float32)), axis=(1, 2), keepdims=True)
    current = (blocks.astype(jnp.float32) / (jnp.sqrt(squares) + 1e-07)).astype(jnp.bfloat16)
    for repeat in range(NS_ITERS):
        gram_block = jnp.einsum(
            "mdi,mdj->mij", current, current, preferred_element_type=jnp.float32
        ).astype(jnp.bfloat16)
        square = jnp.einsum(
            "mij,mjk->mik", gram_block, gram_block, preferred_element_type=jnp.float32
        )
        polynomial = (quintic_b * gram_block.astype(jnp.float32) + quintic_c * square).astype(
            jnp.bfloat16
        )
        product = jnp.einsum(
            "mdi,mij->mdj", current, polynomial, preferred_element_type=jnp.float32
        )
        current = (quintic_a * current.astype(jnp.float32) + product).astype(jnp.bfloat16)
    return current


def body(gradients, momentum, params, outer_moment, shadow):
    scale_step = 0.2 * math.sqrt(D)
    shard_count = lax.axis_size("shard")
    replica_count = lax.axis_size("replica")
    moment_now = momentum[0]
    updates = []
    for position in range(INNER):
        grad_now = gradients[0, position].astype(jnp.float32)
        moment_now = inner_beta * moment_now + grad_now
        updates.append((grad_now + inner_beta * moment_now).astype(jnp.bfloat16))
    owned_total = None
    stacked = jnp.stack(updates)
    owned = lax.all_to_all(stacked, "shard", split_axis=1, concat_axis=2, tiled=True)
    orthos = newton_schulz(owned.reshape((-1,) + owned.shape[2:])).reshape(owned.shape)
    owned_total = scale_step * orthos[0].astype(jnp.float32)
    position = 1
    owned_total = owned_total + scale_step * orthos[position].astype(jnp.float32)
    mat_count = owned_total.shape[0]
    rows_each = owned_total.shape[1] // (shard_count * replica_count)
    width = owned_total.shape[2]
    grouped = owned_total.reshape((mat_count, shard_count, replica_count, rows_each, width))
    reduced = sum_at_owner(grouped.astype(jnp.bfloat16), "replica", 2)
    reduced = reduced.reshape((mat_count, shard_count, rows_each, width))
    placed = lax.all_to_all(
        reduced.astype(jnp.bfloat16), "shard", split_axis=1, concat_axis=0, tiled=True
    ).astype(reduced.dtype)
    summed = placed.reshape((mat_count * shard_count, rows_each, width))
    outer_delta = summed / replica_count
    new_outer = outer_mu * outer_moment + outer_delta
    new_params = params - outer_rate * (outer_delta + outer_mu * new_outer)
    new_shadow = shadow_decay * shadow + (1.0 - shadow_decay) * new_params
    return (new_params, new_outer, new_shadow, moment_now[None])


def solution(mesh):
    in_specs = (
        P("replica", None, None, "shard", None),
        P("replica", None, "shard", None),
        P(None, ("shard", "replica"), None),
        P(None, ("shard", "replica"), None),
        P(None, ("shard", "replica"), None),
    )
    out_specs = (
        P(None, ("shard", "replica"), None),
        P(None, ("shard", "replica"), None),
        P(None, ("shard", "replica"), None),
        P("replica", None, "shard", None),
    )
    return jax.shard_map(body, mesh=mesh, in_specs=in_specs, out_specs=out_specs, check_vma=False)
```

profile of v0, /device:TPU:2, one launch (start us, length us, event | category | flops | bytes accessed | tf_op | source)
XLA Modules:
  0.0 101.9 jit_solution(3864957524999742524)
XLA Ops:
  0.6 2.9 %fusion.14 = (f32[1,64,16,256]{3,2,1,0:T(8,128)}, bf16[1,64,16,256]{3,2,0,1:T(8,128)(2,1)S(1)}, bf16[1,64,16,256]{3,2,0,1:T(8,128)(2,1)S(1)}) fusion(f32[1,64,16,256]{3,2,1,0:T(8,128)} %param.6, bf16[1,2,64,16,256]{4,3,2,1,0:T(8,128)(2,1)} %param.5), kind=kLoop, calls=%fused_computation.38 | loop fusion | flops 2883584 | bytes 4194304
  3.5 0.1 pad_maximum_fusion
  3.6 46.8 %all_to_all.23 = bf16[2,64,16,256]{3,2,0,1:T(8,128)(2,1)S(1)} all-to-all(bf16[2,64,16,256]{3,2,0,1:T(8,128)(2,1)S(1)} %pad_maximum_fusion), channel_id=1, replica_groups=mesh['replica'=8,'shard'=64] {'shard'}, dimensions={1} | all-to-all | bytes 2097152 | tf_op jit(solution)/shard_map/all_to_all | solution.py:62
  50.4 0.4 multiply_reduce_fusion
  50.8 0.3 copy.15
  51.1 0.2 fusion
  51.3 0.5 convolution_convert_fusion.4
  51.9 0.6 add_convert_fusion.4
  52.5 0.5 convolution_convert_fusion.3
  53.0 0.6 add_convert_fusion.3
  53.7 0.5 convolution_convert_fusion.2
  54.2 0.6 add_convert_fusion.2
  54.9 0.5 convolution_convert_fusion.1
  55.4 0.6 add_convert_fusion.1
  56.0 0.5 convolution_convert_fusion
  56.6 0.6 add_convert_fusion
  57.2 0.2 multiply_convert_fusion
  57.4 0.0 copy-start
  57.4 0.2 convert_element_type.209
  57.6 0.4 copy.29
  58.0 23.1 %all_to_all.24 = bf16[8,1,64,1,2,256]{5,4,2,3,1,0:T(2,128)(2,1)S(1)} all-to-all(bf16[8,1,64,1,2,256]{5,4,2,3,1,0:T(2,128)(2,1)S(1)} %bitcast.65), channel_id=1, replica_groups=mesh['replica'=8,'shard'=64] {'replica'}, dimensions={0} | all-to-all | bytes 1048576 | tf_op jit(solution)/shard_map/all_to_all | solution.py:26
  81.1 0.5 reduce_sum.22
  81.6 19.3 %all_to_all.25 = bf16[1,64,2,256]{3,2,0,1:T(2,128)(2,1)S(1)} all-to-all(bf16[1,64,2,256]{3,2,0,1:T(2,128)(2,1)S(1)} %bitcast.66), channel_id=1, replica_groups=mesh['replica'=8,'shard'=64] {'shard'}, dimensions={1} | all-to-all | bytes 131072 | tf_op jit(solution)/shard_map/all_to_all | solution.py:73
  100.9 1.0 multiply_add_fusion
  (6 shorter events, 0.0 us)
Async XLA Ops:
  57.4 43.5 %copy-start = (f32[64,2,256]{2,1,0:T(2,128)S(1)}, f32[64,2,256]{2,1,0:T(2,128)}, u32[]{:S(2)}) copy-start(f32[64,2,256]{2,1,0:T(2,128)} %param.9) | copy-start | bytes 393220
  57.4 43.5 %copy-start.1 = (f32[64,2,256]{2,1,0:T(2,128)S(1)}, f32[64,2,256]{2,1,0:T(2,128)}, u32[]{:S(2)}) copy-start(f32[64,2,256]{2,1,0:T(2,128)} %param.7) | copy-start | bytes 393220
  57.4 43.5 %copy-start.2 = (f32[64,2,256]{2,1,0:T(2,128)S(1)}, f32[64,2,256]{2,1,0:T(2,128)}, u32[]{:S(2)}) copy-start(f32[64,2,256]{2,1,0:T(2,128)} %param.8) | copy-start | bytes 393220
where the time goes:
time: 102 us
  blocking collectives  89.2 us (87%)
  matrix products  5.78 us (6%)
  other arithmetic  5.3 us (5%)
    all_to_all x1, blocking collectives, body(): lax.all_to_all(stacked, 'shard', split_axis=1, concat_axis=2, tiled=True)  46.8 us
    all_to_all x1, blocking collectives, sum_at_owner(): tiles = lax.all_to_all(split_up(shard, dim, size), axis, 0, 0, tiled=True)  23.1 us
    all_to_all x1, blocking collectives, body(): lax.all_to_all(reduced.astype(jnp.bfloat16), 'shard', split_axis=1, conca...  19.3 us
    dot_general x5, matrix products, newton_schulz(): jnp.einsum('mdi,mij->mdj', current, polynomial, preferred_element_type=jn...  3.18 us
    unnamed x1, other arithmetic  2.85 us
    dot_general x5, matrix products, newton_schulz(): jnp.einsum('mdi,mdj->mij', current, current, preferred_element_type=jnp.f...  2.6 us

commit v1 on v0

--- a/solution.py
+++ b/solution.py
@@ -59,7 +59,11 @@
         updates.append((grad_now + inner_beta * moment_now).astype(jnp.bfloat16))
     owned_total = None
     stacked = jnp.stack(updates)
-    owned = lax.all_to_all(stacked, "shard", split_axis=1, concat_axis=2, tiled=True)
+    prior = lax.psum(1, axis_name="shard")
+    h_now = jnp.split(stacked, prior, axis=1)
+    r1 = jnp.stack(h_now)
+    current_arr = lax.all_to_all(r1, axis_name="shard", split_axis=0, concat_axis=0)
+    owned = jnp.concatenate(current_arr, axis=2)
     orthos = newton_schulz(owned.reshape((-1,) + owned.shape[2:])).reshape(owned.shape)
     owned_total = scale_step * orthos[0].astype(jnp.float32)
     position = 1

time: 102 us -> 103 us (level)
    convert_element_type x0 -> x2, other arithmetic: none -> 3.17 us  [the longest x1 2.89 us: body(): updates.append((grad_now + inner_beta * moment_now).astype(jnp.bfloat16))]
    unnamed x1 -> x63, other arithmetic: 2.85 us -> 0.23 us
where the time goes in v1:
time: 103 us
  blocking collectives  89.2 us (87%)
  matrix products  5.78 us (6%)
  other arithmetic  5.77 us (6%)
  between operations  1.26 us (1%)
    all_to_all x1, blocking collectives, body(): lax.all_to_all(r1, axis_name='shard', split_axis=0, concat_axis=0)  46.8 us
    all_to_all x1, blocking collectives, sum_at_owner(): tiles = lax.all_to_all(split_up(shard, dim, size), axis, 0, 0, tiled=True)  23.1 us
    all_to_all x1, blocking collectives, body(): lax.all_to_all(reduced.astype(jnp.bfloat16), 'shard', split_axis=1, conca...  19.3 us
    dot_general x5, matrix products, newton_schulz(): jnp.einsum('mdi,mij->mdj', current, polynomial, preferred_element_type=jn...  3.18 us
    convert_element_type x1, other arithmetic, body(): updates.append((grad_now + inner_beta * moment_now).astype(jnp.bfloat16))  2.89 us
    dot_general x5, matrix products, newton_schulz(): jnp.einsum('mdi,mdj->mij', current, current, preferred_element_type=jnp.f...  2.61 us

profile of v1, /device:TPU:2, one launch (start us, length us, event | category | flops | bytes accessed | tf_op | source)
XLA Modules:
  0.0 102.8 jit_solution(5966478502687264438)
XLA Ops:
  0.6 2.9 %fusion.13 = (bf16[1,64,16,256]{3,2,1,0:T(8,128)(2,1)S(1)}, f32[1,64,16,256]{3,2,1,0:T(8,128)}, bf16[1,64,16,256]{3,2,1,0:T(8,128)(2,1)S(1)}) fusion(bf16[1,2,64,16,256]{4,3,2,1,0:T(8,128)(2,1)} %param.5, f32[1,64,16,256]{3,2,1,0:T(8,128)} %param.6), kind=kLoop, calls=%fused_computation.161 | loop fusion | flops 2883584 | bytes 4194304 | tf_op jit(solution)/shard_map/convert_element_type | solution.py:59
  4.2 46.8 %all_to_all.19 = bf16[64,2,1,16,256]{4,3,1,2,0:T(8,128)(2,1)S(1)} all-to-all(bf16[64,2,1,16,256]{4,3,1,2,0:T(8,128)(2,1)S(1)} %constant_dynamic-update-slice_fusion), channel_id=1, replica_groups=mesh['replica'=8,'shard'=64] {'shard'}, dimensions={0} | all-to-all | bytes 2097152 | tf_op jit(solution)/shard_map/all_to_all | solution.py:65
  51.1 0.4 fusion
  51.5 0.3 convert_bitcast_fusion
  51.8 0.2 copy.141
  52.0 0.3 divide_convert_fusion
  52.2 0.5 convolution_convert_fusion.4
  52.8 0.6 add_convert_fusion.4
  53.4 0.5 convolution_convert_fusion.3
  53.9 0.6 add_convert_fusion.3
  54.6 0.5 convolution_convert_fusion.2
  55.1 0.6 add_convert_fusion.2
  55.8 0.5 convolution_convert_fusion.1
  56.3 0.6 add_convert_fusion.1
  56.9 0.5 convolution_convert_fusion
  57.5 0.6 add_convert_fusion
  58.1 0.2 multiply_convert_fusion
  58.3 0.0 copy-start
  58.3 0.2 convert_element_type.213
  58.5 0.4 copy.217
  58.9 23.1 %all_to_all.20 = bf16[8,1,64,1,2,256]{5,4,2,3,1,0:T(2,128)(2,1)S(1)} all-to-all(bf16[8,1,64,1,2,256]{5,4,2,3,1,0:T(2,128)(2,1)S(1)} %bitcast.308), channel_id=1, replica_groups=mesh['replica'=8,'shard'=64] {'replica'}, dimensions={0} | all-to-all | bytes 1048576 | tf_op jit(solution)/shard_map/all_to_all | solution.py:26
  82.0 0.5 reduce_sum.22
  82.5 19.3 %all_to_all.21 = bf16[1,64,2,256]{3,2,0,1:T(2,128)(2,1)S(1)} all-to-all(bf16[1,64,2,256]{3,2,0,1:T(2,128)(2,1)S(1)} %bitcast.309), channel_id=1, replica_groups=mesh['replica'=8,'shard'=64] {'shard'}, dimensions={1} | all-to-all | bytes 131072 | tf_op jit(solution)/shard_map/all_to_all | solution.py:77
  101.8 1.0 multiply_add_fusion
  (70 shorter events, 0.3 us)
Async XLA Ops:
  58.3 43.5 %copy-start = (f32[64,2,256]{2,1,0:T(2,128)S(1)}, f32[64,2,256]{2,1,0:T(2,128)}, u32[]{:S(2)}) copy-start(f32[64,2,256]{2,1,0:T(2,128)} %param.9) | copy-start | bytes 393220
  58.3 43.5 %copy-start.1 = (f32[64,2,256]{2,1,0:T(2,128)S(1)}, f32[64,2,256]{2,1,0:T(2,128)}, u32[]{:S(2)}) copy-start(f32[64,2,256]{2,1,0:T(2,128)} %param.7) | copy-start | bytes 393220
  58.3 43.5 %copy-start.2 = (f32[64,2,256]{2,1,0:T(2,128)S(1)}, f32[64,2,256]{2,1,0:T(2,128)}, u32[]{:S(2)}) copy-start(f32[64,2,256]{2,1,0:T(2,128)} %param.8) | copy-start | bytes 393220
